TPU v7x, 32 devices: a whole 2x2x4 slice. The times are simulated.
32 devices in a mesh: ctx: 8 (over z, x), ch: 4 (over y, core).
Axes of the slice: x: 2, y: 2, z: 4, core: 2. Of those that a mesh axis runs over, the one named last changes fastest.
Arguments:
- tokens: bfloat16 [2048, 4096], P('ctx', 'ch'), may hold values from -6 to 6
- in_weight: bfloat16 [4096, 3, 4096], P('ch', None, 'ctx'), may hold values from -0.09375 to 0.09375
- short_filter: float32 [4096, 3, 3], P('ch'), may hold values from -3 to 3
- decay_rates: float32 [4096, 16], P('ch'), may hold values from 0.00024414062 to 0.05
- residues: float32 [4096, 16], P('ch'), may hold values from -1.5 to 1.5
- skip_gain: float32 [4096], P('ch'), may hold values from -4 to 4
- out_weight: bfloat16 [4096, 4096], P(None, 'ch'), may hold values from -0.09375 to 0.09375
Outputs:
- mixed: bfloat16 [2048, 4096], P('ctx', 'ch')
All inputs are finite; a program needn't handle non-finite values.
Results may differ from a plain program's by a relative error of at most 0.02.
Values may be sent and summed in bfloat16 or wider, within the bound.
A program may use at most 320 MiB of HBM per device.

v0:
```python
import jax
import jax.numpy as jnp
from jax import lax
from jax.sharding import PartitionSpec as P

HIGHEST = lax.Precision.HIGHEST


def shifted(x, axis, by):
    size = lax.axis_size(axis)
    pairs = [(i, i + by) for i in range(size) if 0 <= i + by < size]
    return lax.ppermute(x, axis, pairs)


def local_conv(product, decay_rates, residues, span):
    chans, length = product.shape
    blocks = length // span
    mode_gain = residues * jnp.sqrt(-jnp.expm1(-2.0 * decay_rates))
    offsets = jnp.arange(span).astype(jnp.float32)
    falling = mode_gain[:, :, None] * jnp.exp(-decay_rates[:, :, None] * offsets)
    rising = jnp.exp(decay_rates[:, :, None] * offsets)
    toeplitz = jnp.einsum("cnt,cns->cts", falling, rising, precision=HIGHEST)
    lower = offsets[:, None] >= offsets[None, :]
    toeplitz = jnp.where(lower[None], toeplitz, 0.0)
    carry_in = mode_gain[:, :, None] * jnp.exp(-decay_rates[:, :, None] * (offsets + 1.0))
    carry_out = jnp.exp(-decay_rates[:, :, None] * (span - 1.0 - offsets))
    through = jnp.exp(-decay_rates * span)
    pieces = product.reshape(chans, blocks, span).transpose(1, 0, 2).astype(jnp.float32)
    within = jnp.einsum("cts,bcs->bct", toeplitz, pieces, precision=HIGHEST)
    injected = jnp.einsum("cns,bcs->bcn", carry_out, pieces, precision=HIGHEST)

    def advance(state, added):
        return (through * state + added, state)

    state, before = lax.scan(advance, jnp.zeros(decay_rates.shape, jnp.float32), injected)
    results = within + jnp.einsum("cnt,bcn->bct", carry_in, before, precision=HIGHEST)
    return (results.transpose(1, 0, 2).reshape(chans, length), state)


def local(tokens, in_weight, short_filter, decay_rates, residues, skip_gain, out_weight):
    rows_here = tokens.shape[0]
    terms = jnp.einsum(
        "rd,dsc->csr",
        tokens,
        lax.all_gather(in_weight, "ctx", axis=2, tiled=True),
        preferred_element_type=jnp.float32,
    )
    projected = lax.psum_scatter(terms.astype(jnp.bfloat16), "ch", scatter_dimension=0, tiled=True)
    group = projected.shape[0]
    reach = short_filter.shape[2] - 1
    rim = shifted(projected[:, :, rows_here - reach :], "ctx", 1)
    extended = jnp.concatenate([rim, projected], axis=2)
    featured = jnp.zeros(projected.shape, jnp.float32)
    for shift_by in range(reach + 1):
        begin = reach - shift_by
        featured = featured + short_filter[:, :, shift_by, None] * extended[
            :, :, begin : begin + rows_here
        ].astype(jnp.float32)
    query = featured[:, 0]
    product = (featured[:, 1] * featured[:, 2]).astype(jnp.bfloat16)
    count = lax.axis_size("ctx")
    chans = group // count
    sent = product.reshape(count, chans, rows_here)
    whole = lax.all_to_all(sent, "ctx", split_axis=0, concat_axis=2, tiled=True)
    length = whole.shape[2]
    start = lax.axis_index("ctx") * chans
    mine_rates = lax.dynamic_slice_in_dim(decay_rates, start, chans, 0)
    mine_residues = lax.dynamic_slice_in_dim(residues, start, chans, 0)
    full_out, final_state = local_conv(
        whole.reshape(chans, length), mine_rates, mine_residues, min(512, length)
    )
    back = lax.all_to_all(
        full_out.reshape(1, chans, length).astype(jnp.bfloat16),
        "ctx",
        split_axis=2,
        concat_axis=0,
        tiled=True,
    ).astype(jnp.float32)
    convolved = back.reshape(group, rows_here)
    gated = (query * (convolved + skip_gain[:, None] * product.astype(jnp.float32))).astype(
        jnp.bfloat16
    )
    mixed = lax.dot_general(
        lax.all_gather(gated, "ch", axis=0, tiled=True),
        out_weight,
        (((0,), (0,)), ((), ())),
        preferred_element_type=jnp.float32,
    )
    return mixed.astype(jnp.bfloat16)


def solution(mesh):
    in_specs = (
        P("ctx", "ch"),
        P("ch", None, "ctx"),
        P("ch", None, None),
        P("ch", None),
        P("ch", None),
        P("ch"),
        P(None, "ch"),
    )
    out_specs = P("ctx", "ch")
    return jax.shard_map(local, mesh=mesh, in_specs=in_specs, out_specs=out_specs, check_vma=False)
```

profile of v0, /device:TPU:0, one launch (start us, length us, event | category | flops | bytes accessed | tf_op | source)
XLA Modules:
  0.0 852.0 jit_solution(11152898393615489229)
XLA Ops:
  6.5 0.0 copy-start
  6.5 0.0 all-gather.3.cloned.1.call-start
  6.5 4.7 copy.22
  11.3 0.0 all-gather.3.cloned.1.call-update
  11.3 0.0 reduce-scatter.2.cloned.1.call-start
  11.3 483.2 %all-gather.3.cloned.1.call-done = bf16[1024,3,4096]{0,2,1:T(8,128)(2,1)} async-done(((bf16[1024,3,512]{0,2,1:T(8,128)(2,1)}), bf16[1024,3,4096]{0,2,1:T(8,128)(2,1)}) %all-gather.3.cloned.1.call-update) | async-done | bytes 25165840 | tf_op jit(solution)/shard_map/all_gather | solution.py:45
  494.6 0.0 copy-done
  494.6 13.3 %fusion.4 = bf16[4096,3,256]{2,0,1:T(8,128)(2,1)} fusion(bf16[1024,3,4096]{0,2,1:T(8,128)(2,1)} %all-gather.3.cloned.1.call-done, bf16[256,1024]{1,0:T(8,128)(2,1)S(1)} %copy-done), kind=kOutput, calls=%fused_computation.7 | convolution fusion | flops 6445596672 | bytes 31981568 | tf_op jit(solution)/shard_map/rd,dsc->csr/dot_general | solution.py:42
  507.9 0.0 copy-start.4
  507.9 0.0 reduce-scatter.2.cloned.1.call-update
  507.9 0.7 multiply_exponential_fusion
  508.6 0.7 sqrt_multiply_fusion
  509.3 0.0 copy-done.4
  509.4 57.0 %reduce-scatter.2.cloned.1.call-done = bf16[1024,3,256]{2,0,1:T(8,128)(2,1)} async-done(((bf16[4096,3,256]{2,0,1:T(8,128)(2,1)}), bf16[1024,3,256]{2,0,1:T(8,128)(2,1)}) %reduce-scatter.2.cloned.1.call-update) | async-done | bytes 1572880 | tf_op jit(solution)/shard_map/reduce_scatter | solution.py:48
  566.4 0.0 copy-start.3
  566.4 1.5 slice.36
  567.9 0.3 copy.23
  568.2 3.3 collective-permute-start
  571.6 0.1 copy.28
  571.7 0.1 copy.27
  571.8 0.1 copy.26
  571.9 1.1 collective-permute-done
  573.0 0.4 copy.24
  573.4 0.0 copy-done.3
  573.4 2.6 multiply_add_fusion
  576.0 0.0 copy-start.2
  576.1 1.6 copy-done.2
  577.7 0.9 fusion.37
  578.6 6.4 all-to-all-start
  584.9 0.0 all-gather.5.cloned.1.call-start
  585.0 118.0 %fusion.12 = f32[128,512,512]{2,1,0:T(8,128)} fusion(f32[128,16]{1,0:T(8,128)S(1)} %copy.28, f32[512]{0:T(512)S(1)} %iota_convert_fusion, f32[128,16]{1,0:T(8,128)S(1)} %copy.27, f32[128,16]{1,0:T(8,128)S(1)} %copy.26), kind=kOutput, calls=%fused_computation.15 | convolution fusion | flops 6445596672 | bytes 134244352 | tf_op jit(solution)/shard_map/cnt,cns->cts/dot_general | solution.py:22
  703.0 0.2 broadcast_compare_fusion
  703.3 0.0 all-to-all-done
  703.3 0.3 copy.25
  703.6 0.3 reshape_reshape.4
  703.9 2.8 fusion.34
  706.7 0.1 copy.29
  706.8 0.2 while.13
  707.0 0.1 copy.30
  707.1 71.1 %fusion = f32[128,4,512]{2,1,0:T(4,128)S(1)} fusion(f32[128,512,512]{2,1,0:T(8,128)} %fusion.12, pred[512,512]{1,0:T(8,128)(4,1)S(1)} %broadcast_compare_fusion, bf16[128,4,512]{2,1,0:T(4,128)(2,1)S(1)} %reshape_reshape.4), kind=kOutput, calls=%fused_computation.2 | convolution fusion | flops 1644167168 | bytes 136052736 | tf_op jit(solution)/shard_map/cts,bcs->bct/dot_general | solution.py:29
  778.2 2.9 fusion.31
  781.2 0.4 convert_element_type.101
  781.5 0.8 copy.31
  782.3 0.5 broadcast.38
  782.8 11.7 %reduce = bf16[2048,128]{1,0:T(8,128)(2,1)S(1)} reduce(bf16[2048,1,128]{2,1,0:T(2,128)(2,1)S(1)} %bitcast.55, bf16[]{:T(256)} %broadcast.38), dimensions={1}, to_apply=%bitcast.43.reduce_sub_computation | reduce | bytes 1048578
  794.6 0.1 reshape.83
  794.7 0.0 copy-start.5
  794.7 18.5 %all_to_all.24 = bf16[8,2,16384]{2,1,0:T(2,128)(2,1)S(1)} all-to-all(bf16[8,2,16384]{2,1,0:T(2,128)(2,1)S(1)} %reshape.83), channel_id=1, replica_groups=mesh['ctx'=8,'ch'=4] {'ctx'}, dimensions={0} | all-to-all | bytes 1048576 | tf_op jit(solution)/shard_map/all_to_all | solution.py:72
  813.2 0.5 reshape.84
  813.7 0.1 copy.32
  813.8 0.1 convert_bitcast_fusion
  813.9 0.3 copy.33
  814.2 0.0 copy-done.5
  814.2 2.9 fusion.39
  817.1 0.0 all-gather.5.cloned.1.call-update
  817.2 20.9 %all-gather.5.cloned.1.call-done = bf16[4096,256]{1,0:T(8,128)(2,1)} async-done(((bf16[1024,256]{1,0:T(8,128)(2,1)}), bf16[4096,256]{1,0:T(8,128)(2,1)}) %all-gather.5.cloned.1.call-update) | async-done | bytes 2097168 | tf_op jit(solution)/shard_map/all_gather | solution.py:84
  838.0 0.0 copy-start.1
  838.0 7.2 convolution_convert_fusion.1
  845.3 0.0 copy-done.1
  (16 shorter events, 0.1 us)
Async XLA Ops:
  6.5 488.1 %copy-start = (bf16[256,1024]{1,0:T(8,128)(2,1)S(1)}, bf16[256,1024]{1,0:T(8,128)(2,1)}, u32[]{:S(2)}) copy-start(bf16[256,1024]{1,0:T(8,128)(2,1)} %param.9) | copy-start | bytes 1572868
  6.5 488.0 %all-gather.3.cloned.1.call-start = ((), (), s32[]{:S(2)}) async-start(), calls=%async_computation.3 | async-start | bytes 28311552 | tf_op jit(solution)/shard_map/all_gather | solution.py:45
  11.3 555.1 %reduce-scatter.2.cloned.1.call-start = ((), (), s32[]{:S(2)}) async-start(), calls=%async_computation.4 | async-start | bytes 7864320 | tf_op jit(solution)/shard_map/reduce_scatter | solution.py:48
  507.9 1.5 copy-start.4
  566.4 7.0 copy-start.3
  568.2 4.7 collective-permute-start
  576.0 1.6 copy-start.2
  578.6 124.7 %all-to-all-start = ((bf16[8,128,256]{2,1,0:T(8,128)(2,1)}), bf16[8,128,256]{2,1,0:T(8,128)(2,1)S(1)}, u32[]{:S(2)}, u32[]{:S(2)}) async-start(bf16[8,128,256]{2,1,0:T(8,128)(2,1)} %bitcast.3), calls=%async_computation.1 | async-start | bytes 1048576 | tf_op jit(solution)/shard_map/all_to_all | solution.py:64
  584.9 253.1 %all-gather.5.cloned.1.call-start = ((), (), s32[]{:S(2)}) async-start(), calls=%async_computation.5 | async-start | bytes 2621440 | tf_op jit(solution)/shard_map/all_gather | solution.py:84
  794.7 19.5 %copy-start.5 = (f32[1024]{0:T(1024)S(1)}, f32[1024]{0:T(1024)}, u32[]{:S(2)}) copy-start(f32[1024]{0:T(1024)} %param.14) | copy-start | bytes 12292
  838.0 7.2 copy-start.1
Sparse Core Ops, SparseCore 0:
  11.4 483.1 all-gather.2
  508.0 58.3 reduce-scatter.1
  817.3 20.7 all-gather.4
where the time goes:
time: 857 us; the launch traced here: 852 us
  waiting for transfers between devices  562 us (66%)
  matrix products  215 us (25%)
  other arithmetic  20 us (2%)
  blocking collectives  18.5 us (2%)
  between operations  13.6 us (2%)
  local copies, waits for them, and re-layouts  12.5 us (1%)
  starting transfers between devices  9.78 us (1%)
    all_gather x1, waiting for transfers between devices, local(): lax.all_gather(in_weight, 'ctx', axis=2, tiled=True)  483 us
    dot_general x1, matrix products, local_conv(): toeplitz = jnp.einsum('cnt,cns->cts', falling, rising, precision=HIGHEST)  118 us
    dot_general x1, matrix products, local_conv(): within = jnp.einsum('cts,bcs->bct', toeplitz, pieces, precision=HIGHEST)  71.1 us
    reduce_scatter x1, waiting for transfers between devices, local(): lax.psum_scatter(terms.astype(jnp.bfloat16), 'ch', scatter_dimension=0, t...  57 us
    all_gather x1, waiting for transfers between devices, local(): lax.all_gather(gated, 'ch', axis=0, tiled=True)  20.9 us
    all_to_all x1, blocking collectives, local(): lax.all_to_all(full_out.reshape(1, chans, length).astype(jnp.bfloat16), '...  18.5 us
  transfers between devices with their start and end apart: 5, of which 4 were waited for; matrix products, arithmetic and copies ran while one was open for 14% of the time, Pallas kernels for 0%

commit v1 on v0

--- a/solution.py
+++ b/solution.py
@@ -4,6 +4,15 @@
 from jax.sharding import PartitionSpec as P
 
 HIGHEST = lax.Precision.HIGHEST
+update_slots = lambda sheet: jnp.concatenate(
+    lax.all_to_all(
+        jnp.stack(jnp.split(sheet, lax.axis_size("ctx"), axis=2)),
+        axis_name="ctx",
+        split_axis=0,
+        concat_axis=0,
+    ),
+    0,
+)
 
 
 def shifted(x, axis, by):
@@ -69,13 +78,7 @@
     full_out, final_state = local_conv(
         whole.reshape(chans, length), mine_rates, mine_residues, min(512, length)
     )
-    back = lax.all_to_all(
-        full_out.reshape(1, chans, length).astype(jnp.bfloat16),
-        "ctx",
-        split_axis=2,
-        concat_axis=0,
-        tiled=True,
-    ).astype(jnp.float32)
+    back = update_slots(full_out.reshape(1, chans, length).astype(jnp.bfloat16)).astype(jnp.float32)
     convolved = back.reshape(group, rows_here)
     gated = (query * (convolved + skip_gain[:, None] * product.astype(jnp.float32))).astype(
         jnp.bfloat16

time: 857 us -> 837 us (0.977)
  other arithmetic: 20 us -> 8.18 us
    unnamed x2 -> x1, other arithmetic: 11.7 us -> 0.01 us
where the time goes in v1:
time: 837 us
  waiting for transfers between devices  562 us (67%)
  matrix products  215 us (26%)
  blocking collectives  18.3 us (2%)
  between operations  13.3 us (2%)
  local copies, waits for them, and re-layouts  10.3 us (1%)
  starting transfers between devices  9.78 us (1%)
    all_gather x1, waiting for transfers between devices, local(): lax.all_gather(in_weight, 'ctx', axis=2, tiled=True)  483 us
    dot_general x1, matrix products, local_conv(): toeplitz = jnp.einsum('cnt,cns->cts', falling, rising, precision=HIGHEST)  118 us
    dot_general x1, matrix products, local_conv(): within = jnp.einsum('cts,bcs->bct', toeplitz, pieces, precision=HIGHEST)  71.1 us
    reduce_scatter x1, waiting for transfers between devices, local(): lax.psum_scatter(terms.astype(jnp.bfloat16), 'ch', scatter_dimension=0, t...  57 us
    all_gather x1, waiting for transfers between devices, local(): lax.all_gather(gated, 'ch', axis=0, tiled=True)  20.9 us
    all_to_all x1, blocking collectives, lax.all_to_all(jnp.stack(jnp.split(sheet, lax.axis_size('ctx'), axis=2)),...  18.3 us
  transfers between devices with their start and end apart: 5, of which 4 were waited for; matrix products, arithmetic and copies ran while one was open for 14% of the time, Pallas kernels for 0%

profile of v1, /device:TPU:0, one launch (start us, length us, event | category | flops | bytes accessed | tf_op | source)
XLA Modules:
  0.0 837.0 jit_solution(13044500700583044399)
XLA Ops:
  6.5 0.0 copy-start
  6.5 0.0 all-gather.3.cloned.1.call-start
  6.5 4.7 copy.34
  11.2 0.0 all-gather.3.cloned.1.call-update
  11.3 0.0 reduce-scatter.2.cloned.1.call-start
  11.3 483.2 %all-gather.3.cloned.1.call-done = bf16[1024,3,4096]{0,2,1:T(8,128)(2,1)} async-done(((bf16[1024,3,512]{0,2,1:T(8,128)(2,1)}), bf16[1024,3,4096]{0,2,1:T(8,128)(2,1)}) %all-gather.3.cloned.1.call-update) | async-done | bytes 25165840 | tf_op jit(solution)/shard_map/all_gather | solution.py:54
  494.6 0.0 copy-done
  494.6 13.3 %fusion.4 = bf16[4096,3,256]{2,0,1:T(8,128)(2,1)} fusion(bf16[1024,3,4096]{0,2,1:T(8,128)(2,1)} %all-gather.3.cloned.1.call-done, bf16[256,1024]{1,0:T(8,128)(2,1)S(1)} %copy-done), kind=kOutput, calls=%fused_computation.7 | convolution fusion | flops 6445596672 | bytes 31981568 | tf_op jit(solution)/shard_map/rd,dsc->csr/dot_general | solution.py:51
  507.9 0.0 copy-start.3
  507.9 0.0 reduce-scatter.2.cloned.1.call-update
  507.9 0.7 multiply_exponential_fusion
  508.6 0.7 sqrt_multiply_fusion
  509.3 0.0 copy-done.3
  509.4 57.0 %reduce-scatter.2.cloned.1.call-done = bf16[1024,3,256]{2,0,1:T(8,128)(2,1)} async-done(((bf16[4096,3,256]{2,0,1:T(8,128)(2,1)}), bf16[1024,3,256]{2,0,1:T(8,128)(2,1)}) %reduce-scatter.2.cloned.1.call-update) | async-done | bytes 1572880 | tf_op jit(solution)/shard_map/reduce_scatter | solution.py:57
  566.4 0.0 copy-start.2
  566.4 1.5 slice.36
  567.9 0.3 copy.35
  568.2 3.4 collective-permute-start
  571.6 0.1 copy.40
  571.7 0.1 copy.39
  571.8 0.1 copy.38
  571.9 1.1 collective-permute-done
  573.0 0.4 copy.36
  573.4 0.0 copy-done.2
  573.4 2.6 multiply_add_fusion
  576.0 0.0 copy-start.1
  576.0 1.6 copy-done.1
  577.7 0.9 fusion.37
  578.6 6.3 all-to-all-start
  584.9 0.0 all-gather.5.cloned.1.call-start
  584.9 117.6 %fusion.12 = f32[128,512,512]{2,1,0:T(8,128)} fusion(f32[128,16]{1,0:T(8,128)S(1)} %copy.40, f32[512]{0:T(512)S(1)} %iota_convert_fusion, f32[128,16]{1,0:T(8,128)S(1)} %copy.39, f32[128,16]{1,0:T(8,128)S(1)} %copy.38), kind=kOutput, calls=%fused_computation.15 | convolution fusion | flops 6445596672 | bytes 134244352 | tf_op jit(solution)/shard_map/cnt,cns->cts/dot_general | solution.py:31
  702.5 0.2 broadcast_compare_fusion
  702.7 0.0 all-to-all-done
  702.7 0.3 copy.37
  703.0 0.3 reshape_reshape.4
  703.4 2.8 fusion.34
  706.1 0.1 copy.41
  706.2 0.2 while.13
  706.4 0.1 copy.42
  706.6 71.1 %fusion = f32[128,4,512]{2,1,0:T(4,128)S(1)} fusion(f32[128,512,512]{2,1,0:T(8,128)} %fusion.12, pred[512,512]{1,0:T(8,128)(4,1)S(1)} %broadcast_compare_fusion, bf16[128,4,512]{2,1,0:T(4,128)(2,1)S(1)} %reshape_reshape.4), kind=kOutput, calls=%fused_computation.2 | convolution fusion | flops 1644167168 | bytes 136052736 | tf_op jit(solution)/shard_map/cts,bcs->bct/dot_general | solution.py:38
  777.7 0.0 copy-start.4
  777.7 2.9 fusion.31
  780.6 0.4 convert_element_type.95
  781.2 18.3 %all_to_all.20 = bf16[8,1,128,256]{3,2,1,0:T(8,128)(2,1)S(1)} all-to-all(bf16[8,1,128,256]{3,2,1,0:T(8,128)(2,1)S(1)} %fusion.44), channel_id=1, replica_groups=mesh['ctx'=8,'ch'=4] {'ctx'}, dimensions={0} | all-to-all | bytes 1048576 | tf_op jit(solution)/shard_map/all_to_all | solution.py:8
  799.5 0.0 copy-done.4
  799.5 2.9 fusion.39
  802.4 0.0 all-gather.5.cloned.1.call-update
  802.4 20.9 %all-gather.5.cloned.1.call-done = bf16[4096,256]{1,0:T(8,128)(2,1)} async-done(((bf16[1024,256]{1,0:T(8,128)(2,1)}), bf16[4096,256]{1,0:T(8,128)(2,1)}) %all-gather.5.cloned.1.call-update) | async-done | bytes 2097168 | tf_op jit(solution)/shard_map/all_gather | solution.py:87
  823.3 7.2 convolution_convert_fusion.1
  (24 shorter events, 0.2 us)
Async XLA Ops:
  6.5 488.0 %copy-start = (bf16[256,1024]{1,0:T(8,128)(2,1)S(1)}, bf16[256,1024]{1,0:T(8,128)(2,1)}, u32[]{:S(2)}) copy-start(bf16[256,1024]{1,0:T(8,128)(2,1)} %param.9) | copy-start | bytes 1572868
  6.5 488.0 %all-gather.3.cloned.1.call-start = ((), (), s32[]{:S(2)}) async-start(), calls=%async_computation.3 | async-start | bytes 28311552 | tf_op jit(solution)/shard_map/all_gather | solution.py:54
  11.3 555.1 %reduce-scatter.2.cloned.1.call-start = ((), (), s32[]{:S(2)}) async-start(), calls=%async_computation.4 | async-start | bytes 7864320 | tf_op jit(solution)/shard_map/reduce_scatter | solution.py:57
  507.9 1.5 copy-start.3
  566.4 7.0 copy-start.2
  568.2 4.8 collective-permute-start
  576.0 1.6 copy-start.1
  578.6 124.2 %all-to-all-start = ((bf16[8,128,256]{2,1,0:T(8,128)(2,1)}), bf16[8,128,256]{2,1,0:T(8,128)(2,1)S(1)}, u32[]{:S(2)}, u32[]{:S(2)}) async-start(bf16[8,128,256]{2,1,0:T(8,128)(2,1)} %bitcast.3), calls=%async_computation.1 | async-start | bytes 1048576 | tf_op jit(solution)/shard_map/all_to_all | solution.py:73
  584.9 238.4 %all-gather.5.cloned.1.call-start = ((), (), s32[]{:S(2)}) async-start(), calls=%async_computation.5 | async-start | bytes 2621440 | tf_op jit(solution)/shard_map/all_gather | solution.py:87
  777.7 21.8 %copy-start.4 = (f32[1024]{0:T(1024)S(1)}, f32[1024]{0:T(1024)}, u32[]{:S(2)}) copy-start(f32[1024]{0:T(1024)} %param.14) | copy-start | bytes 12292
Sparse Core Ops, SparseCore 0:
  11.4 483.1 all-gather.2
  508.0 58.3 reduce-scatter.1
  802.6 20.7 all-gather.4
